TPU v7x, 1024 devices: a whole 4x4x32 slice. The times are simulated.
1024 devices in a mesh: grp: 16 (over x, y), dev: 64 (over z, core).
Axes of the slice: x: 4, y: 4, z: 32, core: 2. Of those that a mesh axis runs over, the one named last changes fastest.
Arguments:
- queries: bfloat16 [1024, 3072], P(('grp', 'dev')), may hold values from -480 to 480
- cached_key_rows: bfloat16 [1024, 512, 512], P(('grp', 'dev')), may hold values from -6 to 6
- cached_value_rows: bfloat16 [1024, 512, 512], P(('grp', 'dev')), may hold values from -6 to 6
- incoming_keys: bfloat16 [1024, 512], P(('grp', 'dev')), may hold values from -6 to 6
- incoming_values: bfloat16 [1024, 512], P(('grp', 'dev')), may hold values from -6 to 6
- lengths: int32 [512], P('grp'), may hold values from 64 to 512, as said below
- residual: bfloat16 [512, 6144], P('grp'), may hold values from -6 to 6
- norm_gain: float32 [6144], replicated, may hold values from 0.25 to 1.75
- expert_ids: int32 [512, 2], P('grp'), may hold values from 0 to 7, all different within a row; in each aligned block of 32 rows (0 to 31, 32 to 63, ...) at most 10 rows name the same one
- route_logits: float32 [512, 2], P('grp'), may hold values from -6 to 6
- w_gate: bfloat16 [6144, 65536], P(None, ('dev', 'grp')), may hold values from -0.078125 to 0.078125
- w_up: bfloat16 [6144, 65536], P(None, ('dev', 'grp')), may hold values from -0.078125 to 0.078125
- w_down: bfloat16 [65536, 6144], P(('dev', 'grp')), may hold values from -0.0625 to 0.0625
Outputs:
- moe_out: bfloat16 [512, 6144], P('grp', 'dev')
Inputs may be any that keep to these rules, and one draw needn't show every extreme that they name: `lengths`: A sequence has at least 64 live positions; some sequence has exactly 512. `expert_ids`: each token names 2 different experts; among the tokens of one group (32 aligned rows) no expert is named more than 10 times, a bound that some block reaches.
All inputs are finite; a program needn't handle non-finite values.
Results may differ from a plain program's by a relative error of at most 0.007.
Values may be sent and summed in bfloat16 or wider, within the bound.
A program may use at most 32 MiB of HBM per device.

v0:
```python
import jax
import jax.numpy as jnp
from jax import lax
from jax.sharding import PartitionSpec as P

QUERY_HEADS = 48
KEY_VALUE_HEADS = 8
HEAD_SIZE = 128
E = 8
SHARING_DEVICES = 2


def slot_matrix(id_rows, prob_rows, expert, slot_cap):
    matched = (id_rows == expert).astype(jnp.int32).reshape(-1)
    position = jnp.cumsum(matched) - matched
    slot_hit = (position[None, :] == jnp.arange(slot_cap, dtype=jnp.int32)[:, None]) & (
        matched[None, :] > 0
    )
    slot_hit = slot_hit.astype(jnp.float32).reshape(slot_cap, id_rows.shape[0], id_rows.shape[1])
    return (jnp.sum(slot_hit, axis=2), jnp.sum(slot_hit * prob_rows[None], axis=(1, 2)))


def body(
    queries,
    cached_key_rows,
    cached_value_rows,
    incoming_keys,
    incoming_values,
    lengths,
    residual,
    norm_gain,
    expert_ids,
    route_logits,
    w_gate,
    w_up,
    w_down,
):
    dev_count = lax.axis_size("dev")
    head_local = cached_key_rows.shape[2] // HEAD_SIZE
    query_group_width = QUERY_HEADS // KEY_VALUE_HEADS
    cache_len = cached_key_rows.shape[1]
    score_scale = HEAD_SIZE ** (-0.5)
    seq_here = lax.axis_index("dev") // SHARING_DEVICES
    length_row = lax.dynamic_slice_in_dim(lengths, seq_here, 1)[0]
    query_mat = queries[0].reshape(head_local, query_group_width, HEAD_SIZE)
    key_mat = cached_key_rows[0].reshape(cache_len, head_local, HEAD_SIZE)
    value_mat = cached_value_rows[0].reshape(cache_len, head_local, HEAD_SIZE)
    score_all = (
        jnp.einsum("hgd,thd->hgt", query_mat, key_mat, preferred_element_type=jnp.float32)
        * score_scale
    )
    mask_live = jnp.arange(cache_len, dtype=jnp.int32) < length_row
    score_all = jnp.where(mask_live[None, None, :], score_all, -1e30)
    new_score = (
        jnp.einsum(
            "hgd,hd->hg",
            query_mat,
            incoming_keys[0].reshape(head_local, HEAD_SIZE),
            preferred_element_type=jnp.float32,
        )
        * score_scale
    )
    row_max = jnp.maximum(jnp.max(score_all, axis=-1), new_score)
    exp_all = jnp.exp(score_all - row_max[..., None])
    exp_new = jnp.exp(new_score - row_max)
    denom_all = jnp.sum(exp_all, axis=-1) + exp_new
    attn_weights = (exp_all / denom_all[..., None]).astype(jnp.bfloat16)
    weight_new = (exp_new / denom_all).astype(jnp.bfloat16)
    mixed_out = jnp.einsum(
        "hgt,thd->hgd", attn_weights, value_mat, preferred_element_type=jnp.float32
    )
    mixed_out = mixed_out + weight_new.astype(jnp.float32)[..., None] * incoming_values[0].reshape(
        head_local, 1, HEAD_SIZE
    ).astype(jnp.float32)
    attended = mixed_out.reshape(1, -1).astype(jnp.bfloat16)
    gathered = lax.all_gather(attended, "dev", axis=0, tiled=True)
    heads_all = gathered.reshape(residual.shape)
    summed = residual.astype(jnp.float32) + heads_all.astype(jnp.float32)
    normed = (
        summed * lax.rsqrt(jnp.mean(summed * summed, axis=-1, keepdims=True) + 1e-05) * norm_gain
    ).astype(jnp.bfloat16)
    route_probs = jax.nn.softmax(route_logits, axis=-1)
    expert = lax.axis_index("dev") // (dev_count // E)
    row_cap = min(10, dev_count // SHARING_DEVICES)
    select_all, slot_weight = slot_matrix(expert_ids, route_probs, expert, row_cap)
    picked = jnp.dot(
        select_all.astype(jnp.bfloat16), normed, preferred_element_type=jnp.float32
    ).astype(jnp.bfloat16)
    rows_all = lax.all_gather(picked, "grp", axis=0, tiled=True)
    gate_out = jnp.dot(rows_all, w_gate, preferred_element_type=jnp.float32)
    up_out = jnp.dot(rows_all, w_up, preferred_element_type=jnp.float32)
    hidden = (jax.nn.silu(gate_out) * up_out).astype(jnp.bfloat16)
    columns = lax.all_to_all(w_down, "grp", split_axis=1, concat_axis=0, tiled=True)
    partial_out = jnp.dot(
        lax.all_gather(hidden, "grp", axis=1, tiled=True),
        columns,
        preferred_element_type=jnp.float32,
    )
    expert_out = lax.all_to_all(partial_out, "grp", split_axis=0, concat_axis=1, tiled=True)
    contrib = jnp.dot(
        select_all.T, slot_weight[:, None] * expert_out, precision=lax.Precision.HIGHEST
    )
    return lax.psum_scatter(contrib, "dev", scatter_dimension=1, tiled=True).astype(jnp.bfloat16)


def solution(mesh):
    return jax.shard_map(
        body,
        mesh=mesh,
        in_specs=(
            P(("grp", "dev"), None),
            P(("grp", "dev"), None, None),
            P(("grp", "dev"), None, None),
            P(("grp", "dev"), None),
            P(("grp", "dev"), None),
            P("grp"),
            P("grp", None),
            P(),
            P("grp", None),
            P("grp", None),
            P(None, ("dev", "grp")),
            P(None, ("dev", "grp")),
            P(("dev", "grp"), None),
        ),
        out_specs=P("grp", "dev"),
        check_vma=False,
    )
```

profile of v0, /device:TPU:1, one launch (start us, length us, event | category | flops | bytes accessed | tf_op | source)
XLA Modules:
  0.0 440.0 jit_solution(8918194229774854928)
XLA Ops:
  6.5 1.3 dynamic_slice.3
  7.9 0.6 iota_compare_fusion
  8.5 0.7 reduce_max.18
  9.2 0.7 fusion.18
  9.9 0.7 fusion.17
  10.6 0.7 convert_element_type.82
  11.3 0.7 reduce.1
  12.1 1.2 broadcast_compare_fusion
  13.3 0.1 copy.53
  13.4 0.1 reshape.90
  13.5 0.2 reduce-window_clone.1
  13.7 0.6 broadcast.65
  14.3 0.7 reduce.6
  15.0 0.1 reshape.91
  15.1 0.1 copy.54
  15.2 1.2 reshape_squeeze.14
  16.4 0.8 fusion.14
  17.2 0.3 fusion.20
  17.5 0.2 fusion.10
  17.7 0.1 reshape_squeeze.16
  17.9 0.2 fusion.3
  18.1 72.4 %all-gather = bf16[64,1,3072]{2,1,0:T(2,128)(2,1)S(1)} all-gather(bf16[1,1,3072]{2,1,0:T(2,128)(2,1)S(1)} %reshape.94), channel_id=1, replica_groups=mesh['grp'=16,'dev'=64] {'dev'}, dimensions={0}, use_global_device_ids=true | all-gather | bytes 399360 | tf_op jit(solution)/shard_map/all_gather | solution.py:76
  90.5 2.3 convert_reduce_fusion
  92.9 0.0 copy-start.2
  92.9 0.3 reshape.93
  93.1 0.2 multiply_reduce_fusion
  93.4 1.4 select_reduce_fusion
  94.8 1.7 fusion
  96.4 0.0 all-gather.4.cloned.1.call-update
  96.5 1.0 copy.73
  97.5 6.8 %all-to-all-start = ((bf16[64,16,384]{2,0,1:T(8,128)(2,1)}), bf16[64,16,384]{2,0,1:T(8,128)(2,1)S(1)}, u32[]{:S(2)}, u32[]{:S(2)}) async-start(bf16[64,16,384]{2,0,1:T(8,128)(2,1)} %bitcast.33), calls=%async_computation | async-start | bytes 1572864 | tf_op jit(solution)/shard_map/all_to_all | solution.py:93
  104.2 0.0 reduce-scatter.4.cloned.1.call-start
  104.3 66.6 %all-gather.4.cloned.1.call-done = bf16[16,10,6144]{2,1,0:T(8,128)(2,1)} async-done(((bf16[1,10,6144]{2,1,0:T(8,128)(2,1)}), bf16[16,10,6144]{2,1,0:T(8,128)(2,1)}) %all-gather.4.cloned.1.call-update) | async-done | bytes 1966096 | tf_op jit(solution)/shard_map/all_gather | solution.py:89
  170.9 2.9 reshape.97
  173.9 0.8 fusion.21
  174.7 0.3 copy-done.3
  175.0 0.8 fusion.2
  175.8 17.7 %all_gather.11 = bf16[160,1024]{0,1:T(8,128)(2,1)S(1)} all-gather(bf16[160,64]{0,1:T(8,128)(2,1)S(1)} %fusion.2), channel_id=1, replica_groups=mesh['grp'=16,'dev'=64] {'grp'}, dimensions={1}, use_global_device_ids=true | all-gather | bytes 348160 | tf_op jit(solution)/shard_map/all_gather | solution.py:95
  193.5 0.2 copy.57
  193.7 0.1 dot_general.32
  193.8 0.4 fusion.22
  194.2 11.8 %all_to_all.35 = f32[16,10,384]{2,1,0:T(8,128)S(1)} all-to-all(f32[16,10,384]{2,1,0:T(8,128)S(1)} %fusion.22), channel_id=1, replica_groups=mesh['grp'=16,'dev'=64] {'grp'}, dimensions={0} | all-to-all | bytes 491520 | tf_op jit(solution)/shard_map/all_to_all | solution.py:99
  206.0 0.1 copy.59
  206.2 0.1 copy.65
  206.3 6.8 %convolution_bitcast_fusion = f32[6144,32]{1,0:T(8,128)} fusion(f32[10,32]{1,0:T(8,128)S(1)} %get-tuple-element.6, f32[10,6144]{1,0:T(8,128)S(1)} %bitcast.37, f32[10]{0:T(128)S(1)} %copy-done.5), kind=kOutput, calls=%fused_computation | convolution fusion | flops 23654400 | bytes 1033512
  213.1 0.0 reduce-scatter.4.cloned.1.call-update
  213.1 218.6 %reduce-scatter.4.cloned.1.call-done = f32[96,32]{1,0:T(8,128)} async-done(((f32[6144,32]{1,0:T(8,128)}), f32[96,32]{1,0:T(8,128)}) %reduce-scatter.4.cloned.1.call-update) | async-done | bytes 12304
  431.7 1.5 copy.63
  (19 shorter events, 0.1 us)
Async XLA Ops:
  6.5 167.3 %copy-start = (bf16[6144,64]{0,1:T(8,128)(2,1)S(1)}, bf16[6144,64]{0,1:T(8,128)(2,1)}, u32[]{:S(2)}) copy-start(bf16[6144,64]{0,1:T(8,128)(2,1)} %param.23) | copy-start | bytes 2359300
  6.5 11.2 %copy-start.4 = (bf16[1,512,512]{2,1,0:T(8,128)(2,1)S(1)}, bf16[1,512,512]{2,1,0:T(8,128)(2,1)}, u32[]{:S(2)}) copy-start(bf16[1,512,512]{2,1,0:T(8,128)(2,1)} %param.15) | copy-start | bytes 1572868
  6.5 164.4 %all-gather.4.cloned.1.call-start = ((), (), s32[]{:S(2)}) async-start(), calls=%async_computation.3 | async-start | bytes 3342336 | tf_op jit(solution)/shard_map/all_gather | solution.py:89
  18.1 75.0 %copy-start.1 = (bf16[32,6144]{1,0:T(8,128)(2,1)S(1)}, bf16[32,6144]{1,0:T(8,128)(2,1)}, u32[]{:S(2)}) copy-start(bf16[32,6144]{1,0:T(8,128)(2,1)} %param.19) | copy-start | bytes 1179652
  92.9 3.6 copy-start.2
  97.5 96.3 %all-to-all-start = ((bf16[64,16,384]{2,0,1:T(8,128)(2,1)}), bf16[64,16,384]{2,0,1:T(8,128)(2,1)S(1)}, u32[]{:S(2)}, u32[]{:S(2)}) async-start(bf16[64,16,384]{2,0,1:T(8,128)(2,1)} %bitcast.33), calls=%async_computation | async-start | bytes 1572864 | tf_op jit(solution)/shard_map/all_to_all | solution.py:93
  104.2 327.5 %reduce-scatter.4.cloned.1.call-start = ((), (), s32[]{:S(2)}) async-start(), calls=%async_computation.4 | async-start | bytes 3194880
  173.9 1.1 copy-start.3
  193.8 12.5 %copy-start.5 = (f32[10]{0:T(128)S(1)}, f32[10]{0:T(128)}, u32[]{:S(2)}) copy-start(f32[10]{0:T(128)} %get-tuple-element.5) | copy-start | bytes 124
Sparse Core Ops, SparseCore 0:
  96.6 74.2 all-gather.3
  213.2 218.4 reduce-scatter.3
where the time goes:
time: 443 us; the launch traced here: 440 us
  waiting for transfers between devices  285 us (64%)
  blocking collectives  102 us (23%)
  between operations  13.6 us (3%)
  matrix products  11.8 us (3%)
  other arithmetic  10.5 us (2%)
  local copies, waits for them, and re-layouts  10.2 us (2%)
  starting transfers between devices  6.8 us (2%)
    unnamed x3, waiting for transfers between devices  219 us
    all_gather x1, blocking collectives, body(): gathered = lax.all_gather(attended, 'dev', axis=0, tiled=True)  72.4 us
    all_gather x1, waiting for transfers between devices, body(): rows_all = lax.all_gather(picked, 'grp', axis=0, tiled=True)  66.6 us
    all_gather x1, blocking collectives, body(): lax.all_gather(hidden, 'grp', axis=1, tiled=True)  17.7 us
    all_to_all x1, blocking collectives, body(): lax.all_to_all(partial_out, 'grp', split_axis=0, concat_axis=1, tiled=True)  11.8 us
  transfers between devices with their start and end apart: 3, of which 2 were waited for; matrix products, arithmetic and copies ran while one was open for 1% of the time, Pallas kernels for 0%

commit v1 on v0

v1 whole, which is shorter than its diff:
```python
import jax
import jax.numpy as jnp
from jax import lax
from jax.experimental import pallas as pl
from jax.experimental.pallas import tpu as pltpu
from jax.sharding import PartitionSpec as P

BF = jnp.bfloat16
F32 = jnp.float32
I32 = jnp.int32
D = 6144
HALF = 3072
NG = 16
SLICE = 384
CAP = 10
ROWS = 160
MESH = pl.DeviceIdType.MESH


def iota(shape, dim):
    return lax.broadcasted_iota(I32, shape, dim)


def kernel(
    q_ref, kn_ref, vn_ref, len_ref, ids_ref, lg_ref,
    k_hbm, v_hbm, res_hbm, gain_hbm, wg_hbm, wu_hbm, wd_hbm,
    out_ref,
    k_v, v_v, res_v, gain_v,
    qs, res24, att24, sq_send, sq_recv, tok, wgu_r, wd_r,
    pk_send, pk_recv, rs_send, rs_recv, hid_send, hid_recv,
    lr_send, lr_recv, fin_send, fin_recv,
    loc_sem, sq_sem, a_ss, a_rs, l_ss, l_rs, wg_ss, wg_rs, wu_ss, wu_rs, wd_ss, wd_rs,
    pk_ss, pk_rs, rs_ss, rs_rs, hid_ss, hid_rs, lr_ss, lr_rs, fin_ss, fin_rs,
):
    g = lax.axis_index("grp")
    d = lax.axis_index("dev")
    a = d // 8
    part = d % 8
    b = part // 2
    c = d % 2

    def did(gg, dd):
        return (gg, dd)

    def rc(src, dst, ss, rs, dev):
        return pltpu.make_async_remote_copy(
            src_ref=src, dst_ref=dst, send_sem=ss, recv_sem=rs,
            device_id=dev, device_id_type=MESH,
        )

    barrier = pltpu.get_barrier_semaphore()

    def sig(dev):
        pl.semaphore_signal(barrier, inc=1, device_id=dev, device_id_type=MESH)

    def sig_far(k, x):
        sig(did(g, ((a + k) % 8) * 8 + part))
        return x

    def fin_out(k):
        return 2 * part + k // 4, 4 * g + k % 4

    def fin_in(e):
        return d // 4, e * 8 + g // 2

    def is_me(gg, dd):
        return jnp.logical_and(gg == g, dd == d)

    lax.fori_loop(1, 8, sig_far, 0)

    def sig_fin(k, x):
        go, do = fin_out(k)
        gi, di = fin_in(k)

        @pl.when(jnp.logical_not(is_me(go, do)))
        def _():
            sig(did(go, do))

        @pl.when(jnp.logical_not(is_me(gi, di)))
        def _():
            sig(did(gi, di))

        return x

    lax.fori_loop(0, 8, sig_fin, 0)
    d_other = d + 1 - 2 * c

    def sig_line(k, x):
        sig(did(g, a * 8 + ((b + k) % 4) * 2 + c))
        sig(did(g, a * 8 + ((b + k) % 4) * 2 + 1 - c))
        return x

    lax.fori_loop(1, 4, sig_line, 0)

    def sig_xy(k, x):
        sig(did((g + k) % NG, d))
        sig(did((g + k) % NG, d_other))
        return x

    lax.fori_loop(1, NG, sig_xy, 0)
    sig(did(g, d_other))

    half_at = pl.multiple_of(c * HALF, HALF)
    loads = [
        pltpu.make_async_copy(k_hbm, k_v, loc_sem.at[0]),
        pltpu.make_async_copy(v_hbm, v_v, loc_sem.at[1]),
        pltpu.make_async_copy(res_hbm.at[:, pl.ds(half_at, HALF)], res_v, loc_sem.at[2]),
        pltpu.make_async_copy(gain_hbm.at[pl.ds(pl.multiple_of(c * 24, 8), 24)], gain_v, loc_sem.at[3]),
    ]
    for cp in loads:
        cp.start()

    token = d // 2
    length = len_ref[token]
    qs[...] = jnp.zeros_like(qs)
    q_row = q_ref[...].astype(F32)
    for i in range(24):
        qs[8 * (i // 6) + i % 6 : 8 * (i // 6) + i % 6 + 1, :] = q_row[:, 128 * i : 128 * i + 128]
    kn = kn_ref[...].astype(F32)
    vn = vn_ref[...].astype(F32)
    live = iota((8, 512), 1) < length
    scale = 128 ** (-0.5)
    loads[0].wait()
    loads[1].wait()
    for h in range(4):
        cols = slice(128 * h, 128 * h + 128)
        q_h = qs[8 * h : 8 * h + 8, :]
        s = lax.dot_general(
            q_h.astype(BF), k_v[:, cols], (((1,), (1,)), ((), ())), preferred_element_type=F32
        ) * scale
        s = jnp.where(live, s, -1e30)
        s_new = jnp.sum(q_h * kn[:, cols], axis=1, keepdims=True) * scale
        top = jnp.maximum(jnp.max(s, axis=1, keepdims=True), s_new)
        e = jnp.exp(s - top)
        e_new = jnp.exp(s_new - top)
        den = jnp.sum(e, axis=1, keepdims=True) + e_new
        o = jnp.dot((e / den).astype(BF), v_v[:, cols], preferred_element_type=F32)
        o = o + (e_new / den).astype(BF).astype(F32) * vn[:, cols]
        att24[6 * h : 6 * h + 6, :] = o[0:6, :].astype(BF).astype(F32)
    loads[2].wait()
    mine = iota((32, HALF), 0) == token
    res_row = jnp.sum(jnp.where(mine, res_v[...].astype(F32), 0.0), axis=0, keepdims=True)
    for i in range(24):
        res24[i : i + 1, :] = res_row[:, 128 * i : 128 * i + 128]
    summed = att24[...] + res24[...]
    sq = jnp.sum(jnp.sum(summed * summed, axis=1, keepdims=True), axis=0, keepdims=True)
    sq_send[...] = jnp.broadcast_to(sq, (8, 128))

    me_out = jnp.logical_and(g // 2 == part, d // 4 == g)
    pl.semaphore_wait(barrier, 15 * 2 + 1 + 7 + 6 + 16 - 2 * me_out.astype(I32))

    sq_copy = rc(sq_send, sq_recv, sq_sem.at[0], sq_sem.at[1], did(g, d_other))
    sq_copy.start()

    ids = ids_ref[...]
    id0, id1 = ids[0:1, :], ids[1:2, :]
    lg = lg_ref[...]
    l0, l1 = lg[0:1, :], lg[1:2, :]
    lm = jnp.maximum(l0, l1)
    e0, e1 = jnp.exp(l0 - lm), jnp.exp(l1 - lm)
    p0, p1 = e0 / (e0 + e1), e1 / (e0 + e1)
    before = jnp.where(iota((32, 32), 0) < iota((32, 32), 1), 1.0, 0.0).astype(BF)
    own = jnp.where(id0 == a, 1.0, 0.0) + jnp.where(id1 == a, 1.0, 0.0)
    own = jnp.broadcast_to(own, (16, 32))
    own_pos = jnp.dot(own.astype(BF), before, preferred_element_type=F32)
    pick_hot = jnp.where(own_pos == iota((16, 32), 0).astype(F32), own, 0.0)
    at = iota((32, 1024), 1)
    spread = jnp.where(iota((32, 1024), 0) == ((at // 32) % 8) * 4 + at // 256, 1.0, 0.0)
    pick_exp = jnp.dot(pick_hot.astype(BF), spread.astype(BF), preferred_element_type=F32)
    in_tok = iota((16, 1024), 1) % 32
    select = jnp.concatenate(
        [jnp.where(in_tok == j, pick_exp, 0.0).astype(BF) for j in range(24)], axis=0
    )

    loads[3].wait()
    sq_copy.wait_recv()
    total = sq_send[...] + sq_recv[...]
    inv = lax.rsqrt(total[0:1, 0:1] * (1.0 / D) + 1e-05)
    normed = summed * inv * gain_v[...]
    tok[b, a] = jnp.concatenate([normed, jnp.zeros((8, 128), F32)], axis=0).astype(BF)

    def a_copy(k):
        aa = (a + k) % 8
        return rc(tok.at[b, a], tok.at[b, a], a_ss.at[k], a_rs.at[a], did(g, aa * 8 + part))

    def a_wait(k):
        aa = (a + k) % 8
        return rc(tok.at[b, aa], tok.at[b, aa], a_ss.at[k], a_rs.at[aa], did(g, aa * 8 + part))

    for k in (4, 3, 5, 2, 6, 1, 7):
        a_copy(k).start()

    def cut(ref, gg):
        return ref.at[:, pl.ds(pl.multiple_of(SLICE * gg, 128), SLICE)]

    def wg_copy(k, src_g, dst_g):
        return rc(cut(wg_hbm, dst_g), wgu_r.at[src_g, pl.ds(0, 64)], wg_ss.at[k], wg_rs.at[src_g], did(dst_g, d))

    def wu_copy(k, src_g, dst_g):
        return rc(cut(wu_hbm, dst_g), wgu_r.at[src_g, pl.ds(64, 64)], wu_ss.at[k], wu_rs.at[src_g], did(dst_g, d))

    def wd_copy(k, src_g, dst_g):
        return rc(
            cut(wd_hbm, dst_g), wd_r.at[src_g],
            wd_ss.at[k], wd_rs.at[src_g], did(dst_g, d))

    def reshard(k, x):
        wg_copy(k, g, (g + k) % NG).start()
        wu_copy(k, g, (g + k) % NG).start()
        return x

    def reshard_down(k, x):
        wd_copy(k, g, (g + k) % NG).start()
        return x

    lax.fori_loop(1, NG, reshard, 0)
    lax.fori_loop(1, NG, reshard_down, 0)
    wg_own = pltpu.make_async_copy(cut(wg_hbm, g), wgu_r.at[g, pl.ds(0, 64)], loc_sem.at[4])
    wu_own = pltpu.make_async_copy(cut(wu_hbm, g), wgu_r.at[g, pl.ds(64, 64)], loc_sem.at[5])
    wd_own = pltpu.make_async_copy(cut(wd_hbm, g), wd_r.at[g], loc_sem.at[6])
    wg_own.start()
    wu_own.start()
    wd_own.start()

    def a_arrive(k, x):
        a_wait(k).wait_recv()
        return x

    lax.fori_loop(1, 8, a_arrive, 0)

    def l_copy(k):
        return rc(tok.at[b], tok.at[b], l_ss.at[k], l_rs.at[b],
                  did(g, a * 8 + ((b + k) % 4) * 2 + c))

    def l_wait(k):
        bb = (b + k) % 4
        return rc(tok.at[bb], tok.at[bb], l_ss.at[k], l_rs.at[bb], did(g, a * 8 + bb * 2 + c))

    for k in (1, 2, 3):
        l_copy(k).start()
    for k in (1, 2, 3):
        l_wait(k).wait_recv()

    picked = jnp.dot(select, tok[...].reshape(1024, 128), preferred_element_type=F32).astype(BF)
    for k in range(8):
        pk_send[k] = picked[48 * k : 48 * k + 48, :]

    def pk_out(k, x):
        gg = 8 * c + (g + k // 2) % 8
        dd = a * 8 + b * 2 + (c + k) % 2
        cp = rc(pk_send.at[(g + k // 2) % 8], pk_recv.at[g], pk_ss.at[k], pk_rs.at[g], did(gg, dd))

        @pl.when(jnp.logical_not(is_me(gg, dd)))
        def _():
            cp.start()

        @pl.when(is_me(gg, dd))
        def _():
            pk_recv[g] = pk_send[(g + k // 2) % 8]

        return x

    lax.fori_loop(0, 16, pk_out, 0)

    pk_from = a * 8 + b * 2 + g // 8

    def pk_in(k, x):
        gg = (g + k) % NG

        @pl.when(jnp.logical_not(is_me(gg, pk_from)))
        def _():
            rc(pk_send.at[0], pk_recv.at[gg], pk_ss.at[k], pk_rs.at[gg], did(gg, pk_from)).wait_recv()

        return x

    lax.fori_loop(0, NG, pk_in, 0)
    squeeze = jnp.where(
        iota((ROWS, 256), 1) == (iota((ROWS, 256), 0) // CAP) * 16 + iota((ROWS, 256), 0) % CAP, 1.0, 0.0
    ).astype(BF)
    x_rows = jnp.concatenate(
        [
            jnp.dot(
                squeeze, pk_recv[:, 16 * j : 16 * j + 16, :].reshape(256, 128),
                preferred_element_type=F32,
            ).astype(BF)
            for j in range(3)
        ],
        axis=1,
    )

    def gu_in(k, x):
        gg = (g + k) % NG
        wg_copy(k, gg, g).wait_recv()
        wu_copy(k, gg, g).wait_recv()
        return x

    wg_own.wait()
    wu_own.wait()
    lax.fori_loop(1, NG, gu_in, 0)

    def rs_copy(src_g, dst_g):
        return rc(rs_send.at[dst_g], rs_recv.at[src_g], rs_ss.at[dst_g], rs_rs.at[src_g], did(dst_g, d))

    def rs_out(i, x):
        chunk = (g // 4 + i) % 4
        y = lax.dot_general(
            x_rows, wgu_r[pl.ds(4 * chunk, 4)].reshape(512, SLICE), (((1,), (1,)), ((), ())),
            preferred_element_type=F32,
        ).astype(BF)
        for j in range(4):
            rs_send[4 * chunk + j] = y[:, 128 * j : 128 * j + 128]
        for j in range(4):
            gg = 4 * chunk + j

            @pl.when(gg != g)
            def _():
                rs_copy(g, gg).start()

        return x

    lax.fori_loop(0, 4, rs_out, 0)
    rs_recv[g] = rs_send[g]

    def rs_in(k, x):
        rs_copy((g + k) % NG, g).wait_recv()
        return x

    lax.fori_loop(1, NG, rs_in, 0)
    both = jnp.sum(rs_recv[...].astype(F32), axis=0)
    gate, up = both[:, :64], both[:, 64:]
    hidden = (gate / (1.0 + jnp.exp(-gate)) * up)
    hid_send[...] = jnp.concatenate([hidden[:80], hidden[80:]], axis=1).astype(BF)
    hid_recv[g] = hid_send[...]

    def hid_copy(k, src_g, dst_g):
        return rc(hid_send, hid_recv.at[src_g], hid_ss.at[k], hid_rs.at[src_g], did(dst_g, d))

    def hid_out(k, x):
        hid_copy(k, g, (g + k) % NG).start()
        return x

    lax.fori_loop(1, NG, hid_out, 0)
    wd_own.wait()

    def wd_in(k, x):
        wd_copy(k, (g + k) % NG, g).wait_recv()
        return x

    lax.fori_loop(1, NG, wd_in, 0)

    def hid_in(k, x):
        hid_copy(k, (g + k) % NG, g).wait_recv()
        return x

    lax.fori_loop(1, NG, hid_in, 0)
    tops, lows = [], []
    for i in range(8):
        h0, h1 = hid_recv[2 * i], hid_recv[2 * i + 1]
        tops.append(jnp.concatenate([h0[:, :64], h1[:, :64]], axis=1))
        lows.append(jnp.concatenate([h0[:, 64:], h1[:, 64:]], axis=1))
    hid_all = jnp.concatenate(
        [jnp.concatenate(tops, axis=1), jnp.concatenate(lows, axis=1)], axis=0
    )
    down = jnp.dot(hid_all, wd_r[...].reshape(1024, SLICE), preferred_element_type=F32).astype(BF)
    widen = jnp.where(
        jnp.logical_and(
            iota((256, ROWS), 1) == (iota((256, ROWS), 0) // 16) * CAP + iota((256, ROWS), 0) % 16,
            iota((256, ROWS), 0) % 16 < CAP,
        ), 1.0, 0.0,
    ).astype(BF)
    lr_send[...] = jnp.dot(widen, down, preferred_element_type=F32).astype(BF).reshape(8, 32, SLICE)

    def lr_copy(k, src_p, dst_p, dev_p):
        return rc(lr_send.at[dst_p], lr_recv.at[src_p], lr_ss.at[k], lr_rs.at[src_p],
                  did(g, a * 8 + dev_p))

    for k in range(1, 8):
        lr_copy(k, part, (part + k) % 8, (part + k) % 8).start()
    lr_recv[part] = lr_send[part]
    for k in range(1, 8):
        pp = (part + k) % 8
        lr_copy(k, pp, part, pp).wait_recv()
    rows = jnp.sum(lr_recv[...].astype(F32), axis=0)
    for k in range(8):
        piece = rows[16 * (k // 4) : 16 * (k // 4) + 16, 96 * (k % 4) : 96 * (k % 4) + 96]
        fin_send[k] = jnp.concatenate([piece, jnp.zeros((16, 32), F32)], axis=1).astype(BF)

    def fin_go(k, x):
        go, do = fin_out(k)

        @pl.when(jnp.logical_not(is_me(go, do)))
        def _():
            rc(fin_send.at[k], fin_recv.at[a], fin_ss.at[k], fin_rs.at[a], did(go, do)).start()

        @pl.when(is_me(go, do))
        def _():
            fin_recv[a] = fin_send[k]

        return x

    lax.fori_loop(0, 8, fin_go, 0)

    slot = iota((128, 32), 0)
    hit0 = jnp.where(id0 == slot // 16, 1.0, 0.0)
    hit1 = jnp.where(id1 == slot // 16, 1.0, 0.0)
    hits = hit0 + hit1
    places = jnp.dot(hits.astype(BF), before, preferred_element_type=F32)
    combine = jnp.where(places == (slot % 16).astype(F32), hit0 * p0 + hit1 * p1, 0.0)

    def fin_come(e, x):
        gi, di = fin_in(e)

        @pl.when(jnp.logical_not(is_me(gi, di)))
        def _():
            rc(fin_send.at[0], fin_recv.at[e], fin_ss.at[e], fin_rs.at[e], did(gi, di)).wait_recv()

        return x

    lax.fori_loop(0, 8, fin_come, 0)
    result = lax.dot_general(
        combine, fin_recv[...].reshape(128, 128).astype(F32), (((0,), (0,)), ((), ())), precision=lax.Precision.HIGHEST,
        preferred_element_type=F32,
    )
    out_ref[...] = result[:, :96].astype(BF)

    sq_copy.wait_send()

    def a_left(k, x):
        a_copy(k).wait_send()
        return x

    lax.fori_loop(1, 8, a_left, 0)
    for k in (1, 2, 3):
        l_copy(k).wait_send()

    def xy_left(k, x):
        gg = (g + k) % NG
        wg_copy(k, g, gg).wait_send()
        wu_copy(k, g, gg).wait_send()
        wd_copy(k, g, gg).wait_send()
        rs_copy(g, gg).wait_send()
        hid_copy(k, g, gg).wait_send()
        return x

    lax.fori_loop(1, NG, xy_left, 0)

    def pk_left(k, x):
        gg = 8 * c + (g + k // 2) % 8
        dd = a * 8 + b * 2 + (c + k) % 2

        @pl.when(jnp.logical_not(is_me(gg, dd)))
        def _():
            rc(pk_send.at[(g + k // 2) % 8], pk_recv.at[g], pk_ss.at[k], pk_rs.at[g], did(gg, dd)).wait_send()

        return x

    lax.fori_loop(0, 16, pk_left, 0)
    for k in range(1, 8):
        lr_copy(k, part, (part + k) % 8, (part + k) % 8).wait_send()

    def fin_left(k, x):
        go, do = fin_out(k)

        @pl.when(jnp.logical_not(is_me(go, do)))
        def _():
            rc(fin_send.at[k], fin_recv.at[a], fin_ss.at[k], fin_rs.at[a], did(go, do)).wait_send()

        return x

    lax.fori_loop(0, 8, fin_left, 0)


def body(
    queries, cached_key_rows, cached_value_rows, incoming_keys, incoming_values, lengths,
    residual, norm_gain, expert_ids, route_logits, w_gate, w_up, w_down,
):
    vmem = pl.BlockSpec(memory_space=pltpu.VMEM)
    anyw = pl.BlockSpec(memory_space=pl.ANY)
    dma = pltpu.SemaphoreType.DMA
    return pl.pallas_call(
        kernel,
        out_shape=jax.ShapeDtypeStruct((32, 96), BF),
        in_specs=[vmem, vmem, vmem, pl.BlockSpec(memory_space=pltpu.SMEM), vmem, vmem] + [anyw] * 7,
        out_specs=vmem,
        scratch_shapes=[
            pltpu.VMEM((512, 512), BF),
            pltpu.VMEM((512, 512), BF),
            pltpu.VMEM((32, HALF), BF),
            pltpu.VMEM((24, 128), F32),
            pltpu.VMEM((32, 128), F32),
            pltpu.VMEM((24, 128), F32),
            pltpu.VMEM((24, 128), F32),
            pltpu.VMEM((8, 128), F32),
            pltpu.VMEM((8, 128), F32),
            pltpu.VMEM((4, 8, 32, 128), BF),
            pltpu.VMEM((NG, 128, SLICE), BF),
            pltpu.VMEM((NG, 64, SLICE), BF),
            pltpu.VMEM((8, 48, 128), BF),
            pltpu.VMEM((NG, 48, 128), BF),
            pltpu.VMEM((NG, ROWS, 128), BF),
            pltpu.VMEM((NG, ROWS, 128), BF),
            pltpu.VMEM((80, 128), BF),
            pltpu.VMEM((NG, 80, 128), BF),
            pltpu.VMEM((8, 32, SLICE), BF),
            pltpu.VMEM((8, 32, SLICE), BF),
            pltpu.VMEM((8, 16, 128), BF),
            pltpu.VMEM((8, 16, 128), BF),
            dma((7,)), dma((2,)), dma((8,)), dma((8,)), dma((4,)), dma((4,)),
            dma((NG,)), dma((NG,)), dma((NG,)), dma((NG,)), dma((NG,)), dma((NG,)),
            dma((NG,)), dma((NG,)), dma((NG,)), dma((NG,)), dma((NG,)), dma((NG,)),
            dma((8,)), dma((8,)), dma((8,)), dma((8,)),
        ],
        compiler_params=pltpu.CompilerParams(
            collective_id=0, has_side_effects=True, vmem_limit_bytes=67000000
        ),
    )(
        queries, incoming_keys, incoming_values, lengths, expert_ids.T, route_logits.T,
        cached_key_rows.reshape(512, 512), cached_value_rows.reshape(512, 512), residual,
        norm_gain.reshape(48, 128), w_gate.T, w_up.T, w_down,
    )


def solution(mesh):
    return jax.shard_map(
        body,
        mesh=mesh,
        in_specs=(
            P(("grp", "dev"), None),
            P(("grp", "dev"), None, None),
            P(("grp", "dev"), None, None),
            P(("grp", "dev"), None),
            P(("grp", "dev"), None),
            P("grp"),
            P("grp", None),
            P(),
            P("grp", None),
            P("grp", None),
            P(None, ("dev", "grp")),
            P(None, ("dev", "grp")),
            P(("dev", "grp"), None),
        ),
        out_specs=P("grp", "dev"),
        check_vma=False,
    )
```

time: 443 us -> 116 us (0.26)
  waiting for transfers between devices: 285 us -> 0 us
  Pallas kernels: 0 us -> 115 us
  blocking collectives: 102 us -> 0 us
  between operations: 13.6 us -> 0.01 us
  matrix products: 11.8 us -> 0 us
  other arithmetic: 10.5 us -> 0 us
  local copies, waits for them, and re-layouts: 10.2 us -> 1.3 us
  starting transfers between devices: 6.8 us -> 0 us
    unnamed x3 -> x0, waiting for transfers between devices: 219 us -> none
    pallas_call x0 -> x1, Pallas kernels: none -> 115 us  [body(): pl.pallas_call(kernel, out_shape=jax.ShapeDtypeStruct((32, 96), BF), in_s...]
    all_gather x2 -> x0, blocking collectives: 90.1 us -> none  [the longest x1 72.4 us: body(): gathered = lax.all_gather(attended, 'dev', axis=0, tiled=True)]
    all_gather x1 -> x0, waiting for transfers between devices: 66.6 us -> none  [body(): rows_all = lax.all_gather(picked, 'grp', axis=0, tiled=True)]
    all_to_all x1 -> x0, blocking collectives: 11.8 us -> none  [body(): lax.all_to_all(partial_out, 'grp', split_axis=0, concat_axis=1, tiled=True)]
    unnamed x1 -> x0, matrix products: 6.8 us -> none
    all_to_all x1 -> x0, starting transfers between devices: 6.76 us -> none  [body(): lax.all_to_all(w_down, 'grp', split_axis=1, concat_axis=0, tiled=True)]
    dot_general x7 -> x0, matrix products: 5.04 us -> none  [the longest x1 1.68 us: body(): jnp.dot(select_all.astype(jnp.bfloat16), normed, preferred_element_type=j...]
  transfers between devices with their start and end apart: 3 -> 0, of which waited for: 2 -> 0; matrix products, arithmetic and copies ran while one was open for 1% -> 0% of each run, Pallas kernels for 0% -> 0%
where the time goes in v1:
time: 116 us
  Pallas kernels  115 us (99%)
  local copies, waits for them, and re-layouts  1.3 us (1%)
    pallas_call x1, Pallas kernels, body(): pl.pallas_call(kernel, out_shape=jax.ShapeDtypeStruct((32, 96), BF), in_s...  115 us

profile of v1, /device:TPU:1, one launch (start us, length us, event | category | flops | bytes accessed | tf_op | source)
XLA Modules:
  0.0 116.1 jit_solution(7322199923806166942)
XLA Ops:
  0.0 114.8 %shard_map.127 = bf16[32,96]{1,0:T(8,128)(2,1)} custom-call(bf16[1,3072]{1,0:T(2,128)(2,1)} %q_ref.1, bf16[1,512]{1,0:T(2,128)(2,1)} %kn_ref.1, bf16[1,512]{1,0:T(2,128)(2,1)} %vn_ref.1, s32[32]{0:T(128)} %len_ref.1, s32[2,32]{1,0:T(2,128)} %bitcast.12, f32[2,32]{1,0:T(2,128)} %bitcast.13, bf16[512,512]{1,0:T(8,128)(2,1)} %bitcast.9, ...), custom_call_target="tpu_custom_call" | custom-call | tf_op jit(solution)/shard_map/pallas_call | solution.py:480
  114.8 1.3 %copy.15 = bf16[32,96]{1,0:T(8,128)(2,1)} copy(bf16[32,96]{1,0:T(8,128)(2,1)} %shard_map.127) | data formatting | bytes 12288

commit v2 on v1

--- a/solution.py
+++ b/solution.py
@@ -22,15 +22,16 @@
 
 
 def kernel(
-    q_ref, kn_ref, vn_ref, len_ref, ids_ref, lg_ref,
+    q_hbm, kn_hbm, vn_hbm, len_hbm, ids_hbm, lg_hbm,
     k_hbm, v_hbm, res_hbm, gain_hbm, wg_hbm, wu_hbm, wd_hbm,
     out_ref,
+    q_ref, kn_ref, vn_ref, len_ref, ids_ref, lg_ref,
     k_v, v_v, res_v, gain_v,
-    qs, res24, att24, sq_send, sq_recv, tok, wgu_r, wd_r,
-    pk_send, pk_recv, rs_send, rs_recv, hid_send, hid_recv,
+    qs, res24, att24, sq_send, sq_recv, tok, wk, wd_r,
+    agb, gu_send, gu_recv, hid_send, hid_recv,
     lr_send, lr_recv, fin_send, fin_recv,
-    loc_sem, sq_sem, a_ss, a_rs, l_ss, l_rs, wg_ss, wg_rs, wu_ss, wu_rs, wd_ss, wd_rs,
-    pk_ss, pk_rs, rs_ss, rs_rs, hid_ss, hid_rs, lr_ss, lr_rs, fin_ss, fin_rs,
+    loc_sem, sq_sem, a_ss, a_rs, l_ss, l_rs, wk_ss, wk_rs, wd_ss, wd_rs,
+    ag_ss, ag_rs, gu_sem, hid_ss, hid_rs, lr_ss, lr_rs, fin_ss, fin_rs,
 ):
     g = lax.axis_index("grp")
     d = lax.axis_index("dev")
@@ -38,6 +39,8 @@
     part = d % 8
     b = part // 2
     c = d % 2
+    xg = g // 4
+    yg = g % 4
 
     def did(gg, dd):
         return (gg, dd)
@@ -68,33 +71,16 @@
 
     lax.fori_loop(1, 8, sig_far, 0)
 
-    def sig_fin(k, x):
-        go, do = fin_out(k)
-        gi, di = fin_in(k)
-
-        @pl.when(jnp.logical_not(is_me(go, do)))
-        def _():
-            sig(did(go, do))
-
-        @pl.when(jnp.logical_not(is_me(gi, di)))
-        def _():
-            sig(did(gi, di))
-
-        return x
-
-    lax.fori_loop(0, 8, sig_fin, 0)
     d_other = d + 1 - 2 * c
 
     def sig_line(k, x):
         sig(did(g, a * 8 + ((b + k) % 4) * 2 + c))
-        sig(did(g, a * 8 + ((b + k) % 4) * 2 + 1 - c))
         return x
 
     lax.fori_loop(1, 4, sig_line, 0)
 
     def sig_xy(k, x):
         sig(did((g + k) % NG, d))
-        sig(did((g + k) % NG, d_other))
         return x
 
     lax.fori_loop(1, NG, sig_xy, 0)
@@ -107,10 +93,18 @@
         pltpu.make_async_copy(res_hbm.at[:, pl.ds(half_at, HALF)], res_v, loc_sem.at[2]),
         pltpu.make_async_copy(gain_hbm.at[pl.ds(pl.multiple_of(c * 24, 8), 24)], gain_v, loc_sem.at[3]),
     ]
-    for cp in loads:
+    small = [
+        pltpu.make_async_copy(src, dst, loc_sem.at[7 + i])
+        for i, (src, dst) in enumerate([
+            (q_hbm, q_ref), (len_hbm, len_ref), (kn_hbm, kn_ref), (vn_hbm, vn_ref),
+            (ids_hbm, ids_ref), (lg_hbm, lg_ref)])
+    ]
+    for cp in small + loads:
         cp.start()
 
     token = d // 2
+    for cp in small:
+        cp.wait()
     length = len_ref[token]
     qs[...] = jnp.zeros_like(qs)
     q_row = q_ref[...].astype(F32)
@@ -146,8 +140,7 @@
     sq = jnp.sum(jnp.sum(summed * summed, axis=1, keepdims=True), axis=0, keepdims=True)
     sq_send[...] = jnp.broadcast_to(sq, (8, 128))
 
-    me_out = jnp.logical_and(g // 2 == part, d // 4 == g)
-    pl.semaphore_wait(barrier, 15 * 2 + 1 + 7 + 6 + 16 - 2 * me_out.astype(I32))
+    pl.semaphore_wait(barrier, 15 + 1 + 7 + 3)
 
     sq_copy = rc(sq_send, sq_recv, sq_sem.at[0], sq_sem.at[1], did(g, d_other))
     sq_copy.start()
@@ -193,33 +186,30 @@
     def cut(ref, gg):
         return ref.at[:, pl.ds(pl.multiple_of(SLICE * gg, 128), SLICE)]
 
-    def wg_copy(k, src_g, dst_g):
-        return rc(cut(wg_hbm, dst_g), wgu_r.at[src_g, pl.ds(0, 64)], wg_ss.at[k], wg_rs.at[src_g], did(dst_g, d))
-
-    def wu_copy(k, src_g, dst_g):
-        return rc(cut(wu_hbm, dst_g), wgu_r.at[src_g, pl.ds(64, 64)], wu_ss.at[k], wu_rs.at[src_g], did(dst_g, d))
+    mine_half = pl.ds(half_at, HALF)
+    other_half = pl.ds(pl.multiple_of((1 - c) * HALF, HALF), HALF)
+    wk_copies = [
+        rc(ref.at[:, other_half], wk.at[2 + i], wk_ss.at[i], wk_rs.at[i], did(g, d_other))
+        for i, ref in enumerate((wg_hbm, wu_hbm))
+    ]
+    wk_own = [
+        pltpu.make_async_copy(ref.at[:, mine_half], wk.at[i], loc_sem.at[4 + i])
+        for i, ref in enumerate((wg_hbm, wu_hbm))
+    ]
 
     def wd_copy(k, src_g, dst_g):
         return rc(
             cut(wd_hbm, dst_g), wd_r.at[src_g],
             wd_ss.at[k], wd_rs.at[src_g], did(dst_g, d))
 
-    def reshard(k, x):
-        wg_copy(k, g, (g + k) % NG).start()
-        wu_copy(k, g, (g + k) % NG).start()
-        return x
-
     def reshard_down(k, x):
         wd_copy(k, g, (g + k) % NG).start()
         return x
 
-    lax.fori_loop(1, NG, reshard, 0)
+    for cp in wk_copies + wk_own:
+        cp.start()
     lax.fori_loop(1, NG, reshard_down, 0)
-    wg_own = pltpu.make_async_copy(cut(wg_hbm, g), wgu_r.at[g, pl.ds(0, 64)], loc_sem.at[4])
-    wu_own = pltpu.make_async_copy(cut(wu_hbm, g), wgu_r.at[g, pl.ds(64, 64)], loc_sem.at[5])
     wd_own = pltpu.make_async_copy(cut(wd_hbm, g), wd_r.at[g], loc_sem.at[6])
-    wg_own.start()
-    wu_own.start()
     wd_own.start()
 
     def a_arrive(k, x):
@@ -242,93 +232,66 @@
         l_wait(k).wait_recv()
 
     picked = jnp.dot(select, tok[...].reshape(1024, 128), preferred_element_type=F32).astype(BF)
-    for k in range(8):
-        pk_send[k] = picked[48 * k : 48 * k + 48, :]
-
-    def pk_out(k, x):
-        gg = 8 * c + (g + k // 2) % 8
-        dd = a * 8 + b * 2 + (c + k) % 2
-        cp = rc(pk_send.at[(g + k // 2) % 8], pk_recv.at[g], pk_ss.at[k], pk_rs.at[g], did(gg, dd))
-
-        @pl.when(jnp.logical_not(is_me(gg, dd)))
-        def _():
+    agb[xg, yg] = picked.reshape(24, 16, 128)
+
+    def side(p, du, dv):
+        dx, dy = (du, dv) if p == 0 else (dv, du)
+        return did(((xg + dx + 4) % 4) * 4 + (yg + dy + 4) % 4, d)
+
+    def ring(p, stage, off, j, n):
+        u, v = (xg, yg) if p == 0 else (yg, xg)
+        js = pl.ds(12 * p + j, n)
+        if stage == 0:
+            u = (u + off + 4) % 4
+            return agb.at[u, v, js] if p == 0 else agb.at[v, u, js]
+        v = (v + off + 4) % 4
+        return agb.at[:, v, js] if p == 0 else agb.at[v, :, js]
+
+    def hop(p, stage, off, j, n, way, number):
+        piece = ring(p, stage, off, j, n)
+        dev = side(p, way, 0) if stage == 0 else side(p, 0, way)
+        at_sem = 4 * stage + number
+        return rc(piece, piece, ag_ss.at[p, at_sem], ag_rs.at[p, at_sem], dev)
+
+    left_ways = []
+    for stage in range(2):
+        for p in range(2):
+            for way, number in ((1, 0), (-1, 1)):
+                cp = hop(p, stage, 0, 0, 12, way, number)
+                cp.start()
+                left_ways.append(cp)
+        for p in range(2):
+            hop(p, stage, -1, 0, 12, 1, 0).wait_recv()
+            cp = hop(p, stage, -1, 0, 6, 1, 2)
             cp.start()
-
-        @pl.when(is_me(gg, dd))
-        def _():
-            pk_recv[g] = pk_send[(g + k // 2) % 8]
-
-        return x
-
-    lax.fori_loop(0, 16, pk_out, 0)
-
-    pk_from = a * 8 + b * 2 + g // 8
-
-    def pk_in(k, x):
-        gg = (g + k) % NG
-
-        @pl.when(jnp.logical_not(is_me(gg, pk_from)))
-        def _():
-            rc(pk_send.at[0], pk_recv.at[gg], pk_ss.at[k], pk_rs.at[gg], did(gg, pk_from)).wait_recv()
-
-        return x
-
-    lax.fori_loop(0, NG, pk_in, 0)
+            left_ways.append(cp)
+            hop(p, stage, 1, 0, 12, -1, 1).wait_recv()
+            cp = hop(p, stage, 1, 6, 6, -1, 3)
+            cp.start()
+            left_ways.append(cp)
+        for p in range(2):
+            hop(p, stage, -2, 0, 6, 1, 2).wait_recv()
+            hop(p, stage, 2, 6, 6, -1, 3).wait_recv()
+
+    for cp in wk_own:
+        cp.wait()
+    for cp in wk_copies:
+        cp.wait_recv()
+    x_rows = jnp.concatenate([agb[:, :, j].reshape(256, 128) for j in range(24)], axis=1)
+    y = lax.dot_general(
+        x_rows, wk[...].reshape(256, HALF), (((1,), (1,)), ((), ())), preferred_element_type=F32
+    )
+    gu_send[...] = y[:, 128:]
+    gu_copy = rc(gu_send, gu_recv, gu_sem.at[0], gu_sem.at[1], did(g, d_other))
+    gu_copy.start()
     squeeze = jnp.where(
         iota((ROWS, 256), 1) == (iota((ROWS, 256), 0) // CAP) * 16 + iota((ROWS, 256), 0) % CAP, 1.0, 0.0
     ).astype(BF)
-    x_rows = jnp.concatenate(
-        [
-            jnp.dot(
-                squeeze, pk_recv[:, 16 * j : 16 * j + 16, :].reshape(256, 128),
-                preferred_element_type=F32,
-            ).astype(BF)
-            for j in range(3)
-        ],
-        axis=1,
-    )
-
-    def gu_in(k, x):
-        gg = (g + k) % NG
-        wg_copy(k, gg, g).wait_recv()
-        wu_copy(k, gg, g).wait_recv()
-        return x
-
-    wg_own.wait()
-    wu_own.wait()
-    lax.fori_loop(1, NG, gu_in, 0)
-
-    def rs_copy(src_g, dst_g):
-        return rc(rs_send.at[dst_g], rs_recv.at[src_g], rs_ss.at[dst_g], rs_rs.at[src_g], did(dst_g, d))
-
-    def rs_out(i, x):
-        chunk = (g // 4 + i) % 4
-        y = lax.dot_general(
-            x_rows, wgu_r[pl.ds(4 * chunk, 4)].reshape(512, SLICE), (((1,), (1,)), ((), ())),
-            preferred_element_type=F32,
-        ).astype(BF)
-        for j in range(4):
-            rs_send[4 * chunk + j] = y[:, 128 * j : 128 * j + 128]
-        for j in range(4):
-            gg = 4 * chunk + j
-
-            @pl.when(gg != g)
-            def _():
-                rs_copy(g, gg).start()
-
-        return x
-
-    lax.fori_loop(0, 4, rs_out, 0)
-    rs_recv[g] = rs_send[g]
-
-    def rs_in(k, x):
-        rs_copy((g + k) % NG, g).wait_recv()
-        return x
-
-    lax.fori_loop(1, NG, rs_in, 0)
-    both = jnp.sum(rs_recv[...].astype(F32), axis=0)
+    gu_copy.wait_recv()
+    both = y[:, :128] + gu_recv[...]
     gate, up = both[:, :64], both[:, 64:]
-    hidden = (gate / (1.0 + jnp.exp(-gate)) * up)
+    hidden = (gate / (1.0 + jnp.exp(-gate)) * up).astype(BF)
+    hidden = jnp.dot(squeeze, hidden, preferred_element_type=F32)
     hid_send[...] = jnp.concatenate([hidden[:80], hidden[80:]], axis=1).astype(BF)
     hid_recv[g] = hid_send[...]
 
@@ -435,26 +398,14 @@
 
     def xy_left(k, x):
         gg = (g + k) % NG
-        wg_copy(k, g, gg).wait_send()
-        wu_copy(k, g, gg).wait_send()
         wd_copy(k, g, gg).wait_send()
-        rs_copy(g, gg).wait_send()
         hid_copy(k, g, gg).wait_send()
         return x
 
     lax.fori_loop(1, NG, xy_left, 0)
 
-    def pk_left(k, x):
-        gg = 8 * c + (g + k // 2) % 8
-        dd = a * 8 + b * 2 + (c + k) % 2
-
-        @pl.when(jnp.logical_not(is_me(gg, dd)))
-        def _():
-            rc(pk_send.at[(g + k // 2) % 8], pk_recv.at[g], pk_ss.at[k], pk_rs.at[g], did(gg, dd)).wait_send()
-
-        return x
-
-    lax.fori_loop(0, 16, pk_left, 0)
+    for cp in left_ways + wk_copies + [gu_copy]:
+        cp.wait_send()
     for k in range(1, 8):
         lr_copy(k, part, (part + k) % 8, (part + k) % 8).wait_send()
 
@@ -480,9 +431,15 @@
     return pl.pallas_call(
         kernel,
         out_shape=jax.ShapeDtypeStruct((32, 96), BF),
-        in_specs=[vmem, vmem, vmem, pl.BlockSpec(memory_space=pltpu.SMEM), vmem, vmem] + [anyw] * 7,
+        in_specs=[anyw] * 13,
         out_specs=vmem,
         scratch_shapes=[
+            pltpu.VMEM((1, HALF), BF),
+            pltpu.VMEM((1, 512), BF),
+            pltpu.VMEM((1, 512), BF),
+            pltpu.SMEM((32,), I32),
+            pltpu.VMEM((2, 32), I32),
+            pltpu.VMEM((2, 32), F32),
             pltpu.VMEM((512, 512), BF),
             pltpu.VMEM((512, 512), BF),
             pltpu.VMEM((32, HALF), BF),
@@ -493,21 +450,20 @@
             pltpu.VMEM((8, 128), F32),
             pltpu.VMEM((8, 128), F32),
             pltpu.VMEM((4, 8, 32, 128), BF),
-            pltpu.VMEM((NG, 128, SLICE), BF),
+            pltpu.VMEM((4, 64, HALF), BF),
             pltpu.VMEM((NG, 64, SLICE), BF),
-            pltpu.VMEM((8, 48, 128), BF),
-            pltpu.VMEM((NG, 48, 128), BF),
-            pltpu.VMEM((NG, ROWS, 128), BF),
-            pltpu.VMEM((NG, ROWS, 128), BF),
+            pltpu.VMEM((4, 4, 24, 16, 128), BF),
+            pltpu.VMEM((256, 128), F32),
+            pltpu.VMEM((256, 128), F32),
             pltpu.VMEM((80, 128), BF),
             pltpu.VMEM((NG, 80, 128), BF),
             pltpu.VMEM((8, 32, SLICE), BF),
             pltpu.VMEM((8, 32, SLICE), BF),
             pltpu.VMEM((8, 16, 128), BF),
             pltpu.VMEM((8, 16, 128), BF),
-            dma((7,)), dma((2,)), dma((8,)), dma((8,)), dma((4,)), dma((4,)),
-            dma((NG,)), dma((NG,)), dma((NG,)), dma((NG,)), dma((NG,)), dma((NG,)),
-            dma((NG,)), dma((NG,)), dma((NG,)), dma((NG,)), dma((NG,)), dma((NG,)),
+            dma((13,)), dma((2,)), dma((8,)), dma((8,)), dma((4,)), dma((4,)),
+            dma((2,)), dma((2,)), dma((NG,)), dma((NG,)),
+            dma((2, 8)), dma((2, 8)), dma((2,)), dma((NG,)), dma((NG,)),
             dma((8,)), dma((8,)), dma((8,)), dma((8,)),
         ],
         compiler_params=pltpu.CompilerParams(

time: 116 us -> 99.9 us (0.86)
  Pallas kernels: 115 us -> 97.7 us
    pallas_call x1, Pallas kernels: 115 us -> 97.7 us  [body(): pl.pallas_call(kernel, out_shape=jax.ShapeDtypeStruct((32, 96), BF), in_s...]
where the time goes in v2:
time: 99.9 us; the launch traced here: 99 us
  Pallas kernels  97.7 us (98%)
  local copies, waits for them, and re-layouts  1.3 us (1%)
    pallas_call x1, Pallas kernels, body(): pl.pallas_call(kernel, out_shape=jax.ShapeDtypeStruct((32, 96), BF), in_s...  97.7 us

profile of v2, /device:TPU:1, one launch (start us, length us, event | category | flops | bytes accessed | tf_op | source)
XLA Modules:
  0.0 99.0 jit_solution(1602097694533862122)
XLA Ops:
  0.0 97.7 %shard_map.127 = bf16[32,96]{1,0:T(8,128)(2,1)} custom-call(bf16[1,3072]{1,0:T(2,128)(2,1)} %q_hbm.1, bf16[1,512]{1,0:T(2,128)(2,1)} %kn_hbm.1, bf16[1,512]{1,0:T(2,128)(2,1)} %vn_hbm.1, s32[32]{0:T(128)} %len_hbm.1, s32[2,32]{1,0:T(2,128)} %bitcast.12, f32[2,32]{1,0:T(2,128)} %bitcast.13, bf16[512,512]{1,0:T(8,128)(2,1)} %bitcast.9, ...), custom_call_target="tpu_custom_call" | custom-call | tf_op jit(solution)/shard_map/pallas_call | solution.py:431
  97.7 1.3 %copy.15 = bf16[32,96]{1,0:T(8,128)(2,1)} copy(bf16[32,96]{1,0:T(8,128)(2,1)} %shard_map.127) | data formatting | bytes 12288

commit v3 on v2

--- a/solution.py
+++ b/solution.py
@@ -56,10 +56,6 @@
     def sig(dev):
         pl.semaphore_signal(barrier, inc=1, device_id=dev, device_id_type=MESH)
 
-    def sig_far(k, x):
-        sig(did(g, ((a + k) % 8) * 8 + part))
-        return x
-
     def fin_out(k):
         return 2 * part + k // 4, 4 * g + k % 4
 
@@ -69,7 +65,11 @@
     def is_me(gg, dd):
         return jnp.logical_and(gg == g, dd == d)
 
-    lax.fori_loop(1, 8, sig_far, 0)
+    agb[...] = jnp.zeros_like(agb)
+    lr_recv[...] = jnp.zeros_like(lr_recv)
+    tok[...] = jnp.zeros_like(tok)
+    sig(did(g, ((a + 1) % 8) * 8 + part))
+    sig(did(g, ((a + 7) % 8) * 8 + part))
 
     d_other = d + 1 - 2 * c
 
@@ -140,7 +140,7 @@
     sq = jnp.sum(jnp.sum(summed * summed, axis=1, keepdims=True), axis=0, keepdims=True)
     sq_send[...] = jnp.broadcast_to(sq, (8, 128))
 
-    pl.semaphore_wait(barrier, 15 + 1 + 7 + 3)
+    pl.semaphore_wait(barrier, 15 + 1 + 2 + 3)
 
     sq_copy = rc(sq_send, sq_recv, sq_sem.at[0], sq_sem.at[1], did(g, d_other))
     sq_copy.start()
@@ -172,16 +172,29 @@
     normed = summed * inv * gain_v[...]
     tok[b, a] = jnp.concatenate([normed, jnp.zeros((8, 128), F32)], axis=0).astype(BF)
 
-    def a_copy(k):
-        aa = (a + k) % 8
-        return rc(tok.at[b, a], tok.at[b, a], a_ss.at[k], a_rs.at[a], did(g, aa * 8 + part))
-
-    def a_wait(k):
-        aa = (a + k) % 8
-        return rc(tok.at[b, aa], tok.at[b, aa], a_ss.at[k], a_rs.at[aa], did(g, aa * 8 + part))
-
-    for k in (4, 3, 5, 2, 6, 1, 7):
-        a_copy(k).start()
+    def tk(bb, aa):
+        return tok.at[bb, aa, pl.ds(0, 24)]
+
+    def a_copy(src_a, way, number):
+        return rc(tk(b, src_a), tk(b, src_a), a_ss.at[number], a_rs.at[src_a],
+                  did(g, ((a + way + 8) % 8) * 8 + part))
+
+    def l_copy(k, bb, aa, to):
+        return rc(tk(bb, aa), tk(bb, aa), l_ss.at[k, aa], l_rs.at[bb, aa], did(g, a * 8 + to * 2 + c))
+
+    leaving = []
+
+    def send(cp):
+        cp.start()
+        leaving.append(cp)
+
+    def to_line(aa):
+        for k in (1, 2, 3):
+            send(l_copy(k, b, aa, (b + k) % 4))
+
+    send(a_copy(a, 1, 0))
+    send(a_copy(a, -1, 4))
+    to_line(a)
 
     def cut(ref, gg):
         return ref.at[:, pl.ds(pl.multiple_of(SLICE * gg, 128), SLICE)]
@@ -212,24 +225,26 @@
     wd_own = pltpu.make_async_copy(cut(wd_hbm, g), wd_r.at[g], loc_sem.at[6])
     wd_own.start()
 
-    def a_arrive(k, x):
-        a_wait(k).wait_recv()
-        return x
-
-    lax.fori_loop(1, 8, a_arrive, 0)
-
-    def l_copy(k):
-        return rc(tok.at[b], tok.at[b], l_ss.at[k], l_rs.at[b],
-                  did(g, a * 8 + ((b + k) % 4) * 2 + c))
-
-    def l_wait(k):
+    for i in (1, 2, 3, 4):
+        left = (a - i + 8) % 8
+        a_copy(left, 1, 0).wait_recv()
+        if i < 4:
+            send(a_copy(left, 1, i))
+        to_line(left)
+        if i < 4:
+            right = (a + i) % 8
+            a_copy(right, -1, 4).wait_recv()
+            if i < 3:
+                send(a_copy(right, -1, 4 + i))
+            to_line(right)
+
+    def l_arrive(i, x):
+        k, aa = 1 + i // 8, i % 8
         bb = (b + k) % 4
-        return rc(tok.at[bb], tok.at[bb], l_ss.at[k], l_rs.at[bb], did(g, a * 8 + bb * 2 + c))
-
-    for k in (1, 2, 3):
-        l_copy(k).start()
-    for k in (1, 2, 3):
-        l_wait(k).wait_recv()
+        l_copy(k, bb, aa, bb).wait_recv()
+        return x
+
+    lax.fori_loop(0, 24, l_arrive, 0)
 
     picked = jnp.dot(select, tok[...].reshape(1024, 128), preferred_element_type=F32).astype(BF)
     agb[xg, yg] = picked.reshape(24, 16, 128)
@@ -238,40 +253,58 @@
         dx, dy = (du, dv) if p == 0 else (dv, du)
         return did(((xg + dx + 4) % 4) * 4 + (yg + dy + 4) % 4, d)
 
-    def ring(p, stage, off, j, n):
+    def piece(p, du, dv, j, n):
         u, v = (xg, yg) if p == 0 else (yg, xg)
+        u, v = (u + du + 4) % 4, (v + dv + 4) % 4
         js = pl.ds(12 * p + j, n)
-        if stage == 0:
-            u = (u + off + 4) % 4
-            return agb.at[u, v, js] if p == 0 else agb.at[v, u, js]
-        v = (v + off + 4) % 4
-        return agb.at[:, v, js] if p == 0 else agb.at[v, :, js]
-
-    def hop(p, stage, off, j, n, way, number):
-        piece = ring(p, stage, off, j, n)
-        dev = side(p, way, 0) if stage == 0 else side(p, 0, way)
-        at_sem = 4 * stage + number
-        return rc(piece, piece, ag_ss.at[p, at_sem], ag_rs.at[p, at_sem], dev)
-
-    left_ways = []
-    for stage in range(2):
+        return agb.at[u, v, js, pl.ds(0, CAP)] if p == 0 else agb.at[v, u, js, pl.ds(0, CAP)]
+
+    def first(p, off, j, n, way, number):
+        ref = piece(p, off, 0, j, n)
+        return rc(ref, ref, ag_ss.at[p, number], ag_rs.at[p, number], side(p, way, 0))
+
+    offs = (0, -1, 1, 2)
+
+    def second(p, which, off, j, n, way, number):
+        ref = piece(p, offs[which], off, j, n)
+        at_sem = 4 + 4 * which + number
+        return rc(ref, ref, ag_ss.at[p, at_sem], ag_rs.at[p, at_sem], side(p, 0, way))
+
+    def both_ways(p, which):
+        send(second(p, which, 0, 0, 12, 1, 0))
+        send(second(p, which, 0, 0, 12, -1, 1))
+
+    def relay(p, which):
+        second(p, which, -1, 0, 12, 1, 0).wait_recv()
+        send(second(p, which, -1, 0, 6, 1, 2))
+        second(p, which, 1, 0, 12, -1, 1).wait_recv()
+        send(second(p, which, 1, 6, 6, -1, 3))
+
+    for p in range(2):
+        send(first(p, 0, 0, 12, 1, 0))
+        send(first(p, 0, 0, 12, -1, 1))
+    for p in range(2):
+        both_ways(p, 0)
+    for p in range(2):
+        first(p, -1, 0, 12, 1, 0).wait_recv()
+        send(first(p, -1, 0, 6, 1, 2))
+        first(p, 1, 0, 12, -1, 1).wait_recv()
+        send(first(p, 1, 6, 6, -1, 3))
+        both_ways(p, 1)
+        both_ways(p, 2)
+    for p in range(2):
+        relay(p, 0)
+    for p in range(2):
+        first(p, -2, 0, 6, 1, 2).wait_recv()
+        first(p, 2, 6, 6, -1, 3).wait_recv()
+        both_ways(p, 3)
+    for which in (1, 2, 3):
         for p in range(2):
-            for way, number in ((1, 0), (-1, 1)):
-                cp = hop(p, stage, 0, 0, 12, way, number)
-                cp.start()
-                left_ways.append(cp)
+            relay(p, which)
+    for which in range(4):
         for p in range(2):
-            hop(p, stage, -1, 0, 12, 1, 0).wait_recv()
-            cp = hop(p, stage, -1, 0, 6, 1, 2)
-            cp.start()
-            left_ways.append(cp)
-            hop(p, stage, 1, 0, 12, -1, 1).wait_recv()
-            cp = hop(p, stage, 1, 6, 6, -1, 3)
-            cp.start()
-            left_ways.append(cp)
-        for p in range(2):
-            hop(p, stage, -2, 0, 6, 1, 2).wait_recv()
-            hop(p, stage, 2, 6, 6, -1, 3).wait_recv()
+            second(p, which, -2, 0, 6, 1, 2).wait_recv()
+            second(p, which, 2, 6, 6, -1, 3).wait_recv()
 
     for cp in wk_own:
         cp.wait()
@@ -331,10 +364,12 @@
             iota((256, ROWS), 0) % 16 < CAP,
         ), 1.0, 0.0,
     ).astype(BF)
-    lr_send[...] = jnp.dot(widen, down, preferred_element_type=F32).astype(BF).reshape(8, 32, SLICE)
+    wide = jnp.dot(widen, down, preferred_element_type=F32).astype(BF)
+    for j in range(3):
+        lr_send[:, :, j] = wide[:, 128 * j : 128 * j + 128].reshape(8, 2, 16, 128)
 
     def lr_copy(k, src_p, dst_p, dev_p):
-        return rc(lr_send.at[dst_p], lr_recv.at[src_p], lr_ss.at[k], lr_rs.at[src_p],
+        return rc(lr_send.at[dst_p, :, :, pl.ds(0, CAP)], lr_recv.at[src_p, :, :, pl.ds(0, CAP)], lr_ss.at[k], lr_rs.at[src_p],
                   did(g, a * 8 + dev_p))
 
     for k in range(1, 8):
@@ -344,9 +379,10 @@
         pp = (part + k) % 8
         lr_copy(k, pp, part, pp).wait_recv()
     rows = jnp.sum(lr_recv[...].astype(F32), axis=0)
+    halves = [jnp.concatenate([rows[i, j] for j in range(3)], axis=1) for i in range(2)]
     for k in range(8):
-        piece = rows[16 * (k // 4) : 16 * (k // 4) + 16, 96 * (k % 4) : 96 * (k % 4) + 96]
-        fin_send[k] = jnp.concatenate([piece, jnp.zeros((16, 32), F32)], axis=1).astype(BF)
+        block = halves[k // 4][:, 96 * (k % 4) : 96 * (k % 4) + 96]
+        fin_send[k] = jnp.concatenate([block, jnp.zeros((16, 32), F32)], axis=1).astype(BF)
 
     def fin_go(k, x):
         go, do = fin_out(k)
@@ -388,14 +424,6 @@
 
     sq_copy.wait_send()
 
-    def a_left(k, x):
-        a_copy(k).wait_send()
-        return x
-
-    lax.fori_loop(1, 8, a_left, 0)
-    for k in (1, 2, 3):
-        l_copy(k).wait_send()
-
     def xy_left(k, x):
         gg = (g + k) % NG
         wd_copy(k, g, gg).wait_send()
@@ -404,7 +432,7 @@
 
     lax.fori_loop(1, NG, xy_left, 0)
 
-    for cp in left_ways + wk_copies + [gu_copy]:
+    for cp in leaving + wk_copies + [gu_copy]:
         cp.wait_send()
     for k in range(1, 8):
         lr_copy(k, part, (part + k) % 8, (part + k) % 8).wait_send()
@@ -457,13 +485,13 @@
             pltpu.VMEM((256, 128), F32),
             pltpu.VMEM((80, 128), BF),
             pltpu.VMEM((NG, 80, 128), BF),
-            pltpu.VMEM((8, 32, SLICE), BF),
-            pltpu.VMEM((8, 32, SLICE), BF),
+            pltpu.VMEM((8, 2, 3, 16, 128), BF),
+            pltpu.VMEM((8, 2, 3, 16, 128), BF),
             pltpu.VMEM((8, 16, 128), BF),
             pltpu.VMEM((8, 16, 128), BF),
-            dma((13,)), dma((2,)), dma((8,)), dma((8,)), dma((4,)), dma((4,)),
+            dma((13,)), dma((2,)), dma((8,)), dma((8,)), dma((4, 8)), dma((4, 8)),
             dma((2,)), dma((2,)), dma((NG,)), dma((NG,)),
-            dma((2, 8)), dma((2, 8)), dma((2,)), dma((NG,)), dma((NG,)),
+            dma((2, 20)), dma((2, 20)), dma((2,)), dma((NG,)), dma((NG,)),
             dma((8,)), dma((8,)), dma((8,)), dma((8,)),
         ],
         compiler_params=pltpu.CompilerParams(

time: 99.9 us -> 91.9 us (0.920)
  Pallas kernels: 97.7 us -> 89.3 us
    pallas_call x1, Pallas kernels: 97.7 us -> 89.3 us  [body(): pl.pallas_call(kernel, out_shape=jax.ShapeDtypeStruct((32, 96), BF), in_s...]
where the time goes in v3:
time: 91.9 us; the launch traced here: 90.6 us
  Pallas kernels  89.3 us (97%)
  local copies, waits for them, and re-layouts  1.3 us (1%)
    pallas_call x1, Pallas kernels, body(): pl.pallas_call(kernel, out_shape=jax.ShapeDtypeStruct((32, 96), BF), in_s...  89.3 us

profile of v3, /device:TPU:1, one launch (start us, length us, event | category | flops | bytes accessed | tf_op | source)
XLA Modules:
  0.0 90.6 jit_solution(14328764398302892797)
XLA Ops:
  0.0 89.3 %shard_map.127 = bf16[32,96]{1,0:T(8,128)(2,1)} custom-call(bf16[1,3072]{1,0:T(2,128)(2,1)} %q_hbm.1, bf16[1,512]{1,0:T(2,128)(2,1)} %kn_hbm.1, bf16[1,512]{1,0:T(2,128)(2,1)} %vn_hbm.1, s32[32]{0:T(128)} %len_hbm.1, s32[2,32]{1,0:T(2,128)} %bitcast.12, f32[2,32]{1,0:T(2,128)} %bitcast.13, bf16[512,512]{1,0:T(8,128)(2,1)} %bitcast.9, ...), custom_call_target="tpu_custom_call" | custom-call | tf_op jit(solution)/shard_map/pallas_call | solution.py:459
  89.3 1.3 %copy.15 = bf16[32,96]{1,0:T(8,128)(2,1)} copy(bf16[32,96]{1,0:T(8,128)(2,1)} %shard_map.127) | data formatting | bytes 12288

commit v4 on v3

--- a/solution.py
+++ b/solution.py
@@ -230,7 +230,12 @@
         a_copy(left, 1, 0).wait_recv()
         if i < 4:
             send(a_copy(left, 1, i))
-        to_line(left)
+        if i == 3:
+            for k in (1, 2, 3):
+                send(rc(tk(b, left), tk(b, left), l_ss.at[k, (a + 4) % 8], l_rs.at[b, left],
+                        did(g, ((a + 1) % 8) * 8 + ((b + k) % 4) * 2 + c)))
+        if i < 4:
+            to_line(left)
         if i < 4:
             right = (a + i) % 8
             a_copy(right, -1, 4).wait_recv()
@@ -331,11 +336,11 @@
     def hid_copy(k, src_g, dst_g):
         return rc(hid_send, hid_recv.at[src_g], hid_ss.at[k], hid_rs.at[src_g], did(dst_g, d))
 
-    def hid_out(k, x):
-        hid_copy(k, g, (g + k) % NG).start()
-        return x
-
-    lax.fori_loop(1, NG, hid_out, 0)
+    steps = sorted(
+        [(dx, dy) for dx in range(4) for dy in range(4) if dx or dy],
+        key=lambda q: -min(q[0], 4 - q[0]) - min(q[1], 4 - q[1]))
+    for k, (dx, dy) in enumerate(steps):
+        send(hid_copy(k, g, ((xg + dx) % 4) * 4 + (yg + dy) % 4))
     wd_own.wait()
 
     def wd_in(k, x):
@@ -427,7 +432,6 @@
     def xy_left(k, x):
         gg = (g + k) % NG
         wd_copy(k, g, gg).wait_send()
-        hid_copy(k, g, gg).wait_send()
         return x
 
     lax.fori_loop(1, NG, xy_left, 0)

time: 91.9 us -> 90.4 us (0.984)
  the two profiles are of different devices: /device:TPU:1 before, /device:TPU:13 now
where the time goes in v4:
time: 90.4 us; the launch traced here: 90.1 us
  Pallas kernels  88.8 us (98%)
  local copies, waits for them, and re-layouts  1.3 us (1%)
    pallas_call x1, Pallas kernels, body(): pl.pallas_call(kernel, out_shape=jax.ShapeDtypeStruct((32, 96), BF), in_s...  88.8 us

profile of v4, /device:TPU:13, one launch (start us, length us, event | category | flops | bytes accessed | tf_op | source)
XLA Modules:
  0.0 90.1 jit_solution(4173645912149180375)
XLA Ops:
  0.0 88.8 %shard_map.127 = bf16[32,96]{1,0:T(8,128)(2,1)} custom-call(bf16[1,3072]{1,0:T(2,128)(2,1)} %q_hbm.1, bf16[1,512]{1,0:T(2,128)(2,1)} %kn_hbm.1, bf16[1,512]{1,0:T(2,128)(2,1)} %vn_hbm.1, s32[32]{0:T(128)} %len_hbm.1, s32[2,32]{1,0:T(2,128)} %bitcast.12, f32[2,32]{1,0:T(2,128)} %bitcast.13, bf16[512,512]{1,0:T(8,128)(2,1)} %bitcast.9, ...), custom_call_target="tpu_custom_call" | custom-call | tf_op jit(solution)/shard_map/pallas_call | solution.py:463
  88.8 1.3 %copy.15 = bf16[32,96]{1,0:T(8,128)(2,1)} copy(bf16[32,96]{1,0:T(8,128)(2,1)} %shard_map.127) | data formatting | bytes 12288
